TPU v7x, 256 devices: a whole 4x4x8 slice. The times are simulated.
256 devices in a mesh: seq: 32 (over y, z), mp: 8 (over x, core).
Axes of the slice: x: 4, y: 4, z: 8, core: 2. Of those that a mesh axis runs over, the one named last changes fastest.
Arguments:
- query_rows: bfloat16 [16384, 8192], P('seq', 'mp'), may hold values from -8 to 8
- key_rows: bfloat16 [16384, 1024], P('seq', 'mp'), may hold values from -8 to 8
- value_rows: bfloat16 [16384, 1024], P('seq', 'mp'), may hold values from -6 to 6
- cotangent: bfloat16 [16384, 8192], P('seq', 'mp'), may hold values from -6 to 6
- router_logits: float32 [16384], P('seq'), may hold values from -8 to 8
- selection: int32 [4096], P('seq'), may hold values from -1 to 511, as said below
Outputs:
- mixed: bfloat16 [16384, 8192], P('seq', 'mp')
- query_grad: bfloat16 [16384, 8192], P('seq', 'mp')
- key_grad: bfloat16 [16384, 1024], P('seq', 'mp')
- value_grad: bfloat16 [16384, 1024], P('seq', 'mp')
- router_grad: float32 [16384], P('seq')
Inputs may be any that keep to these rules, and one draw needn't show every extreme that they name: `selection`: each shard's block of 128 entries lists the local positions of its selected tokens in ascending order, then -1 in the remaining entries; all shards together select exactly 2048 tokens, and some shard selects exactly 128.
All inputs are finite; a program needn't handle non-finite values.
Results may differ from a plain program's by a relative error of at most 0.012.
The roundings to bfloat16 on the way count: a program that leaves them out, or rounds other values in their place, can miss the bound.
Values may be sent and summed in bfloat16 or wider, within the bound.
No kernel may reach another device: no remote copies, remote signals or barrier semaphores. Data moves between devices by JAX's collectives and lax.ppermute only.
A program may use at most 64 MiB of HBM per device.

v0:
```python
import jax
import jax.numpy as jnp
from jax import lax
from jax.sharding import PartitionSpec as P

HEAD_DIM = 128


def place_rows(values_in, targets, tok_rows):
    flat = values_in.reshape(-1, values_in.shape[-1])
    empty = jnp.zeros((tok_rows, flat.shape[-1]), flat.dtype)
    return empty.at[targets.reshape(-1)].set(flat, mode="drop")


def shards(query_rows, key_rows, value_rows, cotangent, router_logits, selection):
    axis_width = lax.axis_size("seq")
    shard_index = lax.axis_index("seq")
    tok_rows = query_rows.shape[0]
    slot_total = selection.shape[0]
    cap_slots = slot_total // axis_width
    block_rows = slot_total // 2
    q_cols = query_rows.shape[1]
    kv_cols = key_rows.shape[1]
    q_heads = q_cols // HEAD_DIM
    kv_heads_dev = kv_cols // HEAD_DIM
    group = q_heads // kv_heads_dev
    scale = HEAD_DIM ** (-0.5)
    picked = selection >= 0
    own_count = jnp.sum(picked.astype(jnp.int32))
    counts = lax.all_gather(own_count.reshape(1), "seq", axis=0, tiled=True)
    offsets = jnp.cumsum(counts) - counts
    lanes = jnp.arange(axis_width, dtype=jnp.int32)
    own_offset = jnp.sum(jnp.where(lanes == shard_index, offsets, 0))
    slot_steps = jnp.arange(cap_slots, dtype=jnp.int32)
    local_index = (
        jnp.mod(lanes - own_offset, axis_width)[:, None] + axis_width * slot_steps[None, :]
    )
    slot_live = local_index < own_count
    positions = jnp.where(slot_live, selection[local_index], tok_rows)
    safe_rows = jnp.minimum(positions, tok_rows - 1)
    live_mask = slot_live[:, :, None]
    router = jax.nn.sigmoid(router_logits[safe_rows])
    cot_rows = cotangent[safe_rows]
    query_send = jnp.where(live_mask, query_rows[safe_rows], 0)
    grad_send = jnp.where(live_mask, router[:, :, None] * cot_rows.astype(jnp.float32), 0.0).astype(
        jnp.bfloat16
    )
    query_recv, grad_recv = (
        lax.all_to_all(query_send, "seq", split_axis=0, concat_axis=0, tiled=True),
        lax.all_to_all(grad_send, "seq", split_axis=0, concat_axis=0, tiled=True),
    )
    row_ids = jnp.arange(block_rows, dtype=jnp.int32)
    query_rank = shard_index + axis_width * row_ids
    shard_ends = offsets + counts
    source = jnp.sum((shard_ends[None, :] <= query_rank[:, None]).astype(jnp.int32), axis=1)
    source_offset = offsets[source]
    first_rank = source_offset + jnp.mod(shard_index - source_offset, axis_width)
    slot_index = source * cap_slots + (query_rank - first_rank) // axis_width

    def compact(received):
        return received.reshape(axis_width * cap_slots, received.shape[2])[slot_index]

    own_rows = jnp.minimum(jnp.where(picked, selection, 0), tok_rows - 1)
    own_pairs = jnp.where(
        picked[:, None], jnp.concatenate([key_rows[own_rows], value_rows[own_rows]], axis=1), 0
    )
    key_set = lax.all_gather(own_pairs, "seq", axis=0, tiled=True)
    key_ids = jnp.arange(axis_width * slot_total, dtype=jnp.int32)
    key_source = key_ids // slot_total
    key_slot = jnp.mod(key_ids, slot_total)
    key_rank = jnp.where(
        key_slot < counts[key_source], offsets[key_source] + key_slot, axis_width * slot_total
    )
    query_block = compact(query_recv)
    grad_block = compact(grad_recv)
    allowed = key_rank[None, :] <= query_rank[:, None]
    contract = (((1,), (1,)), ((), ()))
    weight_list, dscore_list, output_list, dquery_list = ([], [], [], [])
    for head_index in range(q_heads):
        kv_head = head_index // group
        col_start = head_index * HEAD_DIM
        query_head = query_block[:, col_start : col_start + HEAD_DIM]
        grad_head = grad_block[:, col_start : col_start + HEAD_DIM]
        key_head = key_set[:, kv_head * HEAD_DIM : (kv_head + 1) * HEAD_DIM]
        value_head = key_set[:, kv_cols + kv_head * HEAD_DIM : kv_cols + (kv_head + 1) * HEAD_DIM]
        scores = (
            lax.dot_general(query_head, key_head, contract, preferred_element_type=jnp.float32)
            * scale
        )
        top_score = jnp.max(jnp.where(allowed, scores, -jnp.inf), axis=1, keepdims=True)
        expo = jnp.where(allowed, jnp.exp(scores - top_score), 0.0)
        weights = (expo / jnp.sum(expo, axis=1, keepdims=True)).astype(jnp.bfloat16)
        attended = jnp.dot(weights, value_head, preferred_element_type=jnp.float32).astype(
            jnp.bfloat16
        )
        slope = lax.dot_general(grad_head, value_head, contract, preferred_element_type=jnp.float32)
        centre = jnp.sum(
            grad_head.astype(jnp.float32) * attended.astype(jnp.float32), axis=1, keepdims=True
        )
        d_scores = (weights.astype(jnp.float32) * (slope - centre) * scale).astype(jnp.bfloat16)
        dquery_list.append(
            jnp.dot(d_scores, key_head, preferred_element_type=jnp.float32).astype(jnp.bfloat16)
        )
        weight_list.append(weights)
        dscore_list.append(d_scores)
        output_list.append(attended)
    attended_all = jnp.concatenate(output_list, axis=1)
    dquery_all = jnp.concatenate(dquery_list, axis=1)
    key_count = key_set.shape[0]
    weight_stack = jnp.stack(weight_list).reshape(kv_heads_dev, group, block_rows, key_count)
    dscore_stack = jnp.stack(dscore_list).reshape(kv_heads_dev, group, block_rows, key_count)
    query_split = query_block.reshape(block_rows, kv_heads_dev, group, HEAD_DIM)
    grad_split = grad_block.reshape(block_rows, kv_heads_dev, group, HEAD_DIM)
    back_first = offsets + jnp.mod(shard_index - offsets, axis_width)
    back_ranks = back_first[:, None] + axis_width * slot_steps[None, :]
    back_live = (back_ranks < shard_ends[:, None])[:, :, None]
    back_rows = jnp.minimum((back_ranks - shard_index) // axis_width, block_rows - 1)

    def slots_back(rows_in):
        return jnp.where(back_live, rows_in[back_rows], 0)

    key_part = jnp.einsum(
        "hgbk,bhgd->khd", dscore_stack, query_split, preferred_element_type=jnp.float32
    )
    value_part = jnp.einsum(
        "hgbk,bhgd->khd", weight_stack, grad_split, preferred_element_type=jnp.float32
    )
    pair_grads = lax.psum_scatter(
        jnp.concatenate(
            [
                key_part.reshape(lax.axis_size("seq") * slot_total, kv_cols),
                value_part.reshape(lax.axis_size("seq") * slot_total, kv_cols),
            ],
            axis=1,
        ),
        "seq",
        scatter_dimension=0,
        tiled=True,
    ).astype(jnp.bfloat16)
    out_back, dquery_back = (
        lax.all_to_all(slots_back(attended_all), "seq", split_axis=0, concat_axis=0, tiled=True),
        lax.all_to_all(slots_back(dquery_all), "seq", split_axis=0, concat_axis=0, tiled=True),
    )
    own_targets = jnp.where(picked, selection, tok_rows)
    key_grad = place_rows(pair_grads[:, :kv_cols], own_targets, tok_rows)
    value_grad = place_rows(pair_grads[:, kv_cols:], own_targets, tok_rows)
    out_float = out_back.astype(jnp.float32)
    mixed = place_rows((router[:, :, None] * out_float).astype(jnp.bfloat16), positions, tok_rows)
    query_grad = place_rows(dquery_back, positions, tok_rows)
    partial_sums = jnp.sum(cot_rows.astype(jnp.float32) * out_float, axis=2)
    feature_sum = lax.psum(partial_sums, "mp")
    router_terms = (router * (1.0 - router) * feature_sum).reshape(-1)
    router_grad = (
        jnp.zeros((tok_rows,), jnp.float32).at[positions.reshape(-1)].set(router_terms, mode="drop")
    )
    return (mixed, query_grad, key_grad, value_grad, router_grad)


def solution(mesh):
    in_specs = (P("seq", "mp"), P("seq", "mp"), P("seq", "mp"), P("seq", "mp"), P("seq"), P("seq"))
    out_specs = (P("seq", "mp"), P("seq", "mp"), P("seq", "mp"), P("seq", "mp"), P("seq"))
    return jax.shard_map(shards, mesh=mesh, in_specs=in_specs, out_specs=out_specs, check_vma=False)
```

profile of v0, /device:TPU:4, one launch (start us, length us, event | category | flops | bytes accessed | tf_op | source)
XLA Modules:
  0.0 416.3 jit_solution(17175785645465806378)
XLA Ops:
  7.2 1.9 compare_select_fusion.32
  9.8 1.6 gather_fusion.5
  11.3 1.6 gather_fusion.6
  13.7 1.3 dynamic-slice
  15.0 1.4 dynamic-update-slice
  16.4 23.8 %all-reduce = s32[32]{0:T(128)S(1)} all-reduce(s32[32]{0:T(128)S(1)} %dynamic-update-slice), channel_id=1, replica_groups=mesh['seq'=32,'mp'=8] {'seq'}, use_global_device_ids=true, to_apply=%add | all-reduce | flops 32 | bytes 256
  41.9 1.2 gather_fusion
  43.4 0.7 compare_select_fusion.18
  44.3 0.9 gather_fusion.2
  46.2 0.9 broadcast_select_fusion
  47.1 3.9 all-to-all-start
  51.0 0.8 gather_fusion.3
  54.6 4.4 %compare_select_fusion.21 = s32[4096,1]{0,1:T(1,128)S(1)} fusion(s32[]{:T(128)} %bitcast.62, s32[]{:T(128)} %bitcast.63, s32[]{:T(128)} %bitcast.64, s32[]{:T(128)} %bitcast.65, s32[]{:T(128)} %bitcast.66, s32[]{:T(128)} %bitcast.68, s32[]{:T(128)} %bitcast.67), kind=kLoop, calls=%fused_computation.197 | loop fusion | flops 94208 | bytes 16412 | tf_op jit(solution)/shard_map/gather | solution.py:72
  59.0 4.3 %compare_select_fusion.20 = s32[4096,1]{0,1:T(1,128)S(1)} fusion(s32[]{:T(128)} %bitcast.29, s32[]{:T(128)} %bitcast.30, s32[]{:T(128)} %bitcast.31, s32[]{:T(128)} %bitcast.32, s32[]{:T(128)} %bitcast.33, s32[]{:T(128)} %bitcast.35, s32[]{:T(128)} %bitcast.34), kind=kLoop, calls=%fused_computation.196 | loop fusion | flops 94208 | bytes 16412 | tf_op jit(solution)/shard_map/gather | solution.py:72
  63.9 0.7 fusion.133
  64.6 0.7 fusion.131
  65.3 31.4 %fusion.71 = s32[4096]{0:T(1024)S(1)} fusion(pred[4096]{0:T(1024)(128)(4,1)S(1)} %compare_reduce_fusion, pred[4096]{0:T(1024)(128)(4,1)S(1)} %compare_reduce_fusion.1, pred[4096]{0:T(1024)(128)(4,1)S(1)} %compare_reduce_fusion.2, pred[4096]{0:T(1024)(128)(4,1)S(1)} %compare_reduce_fusion.3, pred[4096]{0:T(1024)(128)(4,1)S(1)} %compare_reduce_fusion.4, ...), kind=kLoop, calls=%fused_computation.239 | loop fusion | flops 241664 | bytes 151752 | tf_op jit(solution)/shard_map/jit(_where)/select_n | solution.py:71
  97.6 1.9 convolution_multiply_fusion.1
  102.4 1.4 fusion.41
  103.7 1.9 fusion.49
  108.3 1.2 constant_dynamic-update-slice_fusion.7
  109.5 0.9 constant_dynamic-update-slice_fusion.6
  110.4 0.9 constant_dynamic-update-slice_fusion.5
  111.3 0.9 constant_dynamic-update-slice_fusion.4
  112.2 0.9 constant_dynamic-update-slice_fusion.3
  113.1 0.9 constant_dynamic-update-slice_fusion.2
  114.0 0.9 constant_dynamic-update-slice_fusion.1
  115.0 0.9 constant_dynamic-update-slice_fusion
  115.9 1.6 gather_fusion.7
  117.4 1.8 reshape.804
  119.2 1.9 broadcast_select_fusion.2
  121.1 9.9 %all-to-all-start.1 = ((bf16[32,4,1024]{2,1,0:T(4,128)(2,1)}), bf16[32,4,1024]{2,1,0:T(4,128)(2,1)}, u32[]{:S(2)}, u32[]{:S(2)}) async-start(bf16[32,4,1024]{2,1,0:T(4,128)(2,1)} %broadcast_select_fusion.2), calls=%async_computation.1 | async-start | bytes 524288 | tf_op jit(solution)/shard_map/all_to_all | solution.py:141
  131.0 1.3 gather_fusion.1
  132.4 3.1 gather_fusion.8
  135.5 1.9 reshape.887
  137.4 4.3 %all-to-all-done.1 = bf16[32,4,1024]{2,1,0:T(4,128)(2,1)} async-done(((bf16[32,4,1024]{2,1,0:T(4,128)(2,1)}), bf16[32,4,1024]{2,1,0:T(4,128)(2,1)}, u32[]{:S(2)}, u32[]{:S(2)}) %all-to-all-start.1) | async-done | bytes 262176 | tf_op jit(solution)/shard_map/all_to_all | solution.py:141
  141.8 2.9 fusion.51
  144.7 5.5 %all-to-all-start.2 = ((bf16[32,4,1024]{2,1,0:T(4,128)(2,1)}), bf16[32,4,1024]{2,1,0:T(4,128)(2,1)}, u32[]{:S(2)}, u32[]{:S(2)}) async-start(bf16[32,4,1024]{2,1,0:T(4,128)(2,1)} %get-tuple-element.50), calls=%async_computation.2 | async-start | bytes 524288 | tf_op jit(solution)/shard_map/all_to_all | solution.py:50
  151.1 9.8 %all-to-all-done.2 = bf16[32,4,1024]{2,1,0:T(4,128)(2,1)} async-done(((bf16[32,4,1024]{2,1,0:T(4,128)(2,1)}), bf16[32,4,1024]{2,1,0:T(4,128)(2,1)}, u32[]{:S(2)}, u32[]{:S(2)}) %all-to-all-start.2) | async-done | bytes 262176 | tf_op jit(solution)/shard_map/all_to_all | solution.py:50
  160.9 1.0 reshape.662
  162.8 4.9 %convolution_bitcast_fusion = f32[4096,128]{0,1:T(8,128)S(1)} fusion(bf16[64,8,128]{2,1,0:T(8,128)(2,1)S(1)} %bitcast.167, bf16[8,64,4096]{2,1,0:T(8,128)(2,1)} %copy-done.4), kind=kOutput, calls=%fused_computation.32 | convolution fusion | flops 536870912 | bytes 6422528 | tf_op jit(solution)/shard_map/hgbk,bhgd->khd/dot_general | solution.py:125
  168.0 1.3 bitcast_dynamic-update-slice_fusion.15
  169.3 1.3 bitcast_dynamic-update-slice_fusion.14
  170.6 1.3 bitcast_dynamic-update-slice_fusion.13
  171.9 1.3 bitcast_dynamic-update-slice_fusion.12
  173.2 1.3 bitcast_dynamic-update-slice_fusion.11
  174.5 1.3 bitcast_dynamic-update-slice_fusion.10
  175.8 1.3 bitcast_dynamic-update-slice_fusion.9
  177.1 1.3 bitcast_dynamic-update-slice_fusion.8
  178.4 2.6 convolution_bitcast_fusion.1
  181.1 2.4 pad_maximum_fusion
  183.5 1.4 fusion.33
  184.9 1.4 fusion.32
  188.5 0.9 gather_fusion.10
  189.5 0.9 broadcast_select_fusion.1
  190.4 4.7 %all-to-all-start.3 = ((bf16[32,4,1024]{2,1,0:T(4,128)(2,1)}), bf16[32,4,1024]{2,1,0:T(4,128)(2,1)S(1)}, u32[]{:S(2)}, u32[]{:S(2)}) async-start(bf16[32,4,1024]{2,1,0:T(4,128)(2,1)} %broadcast_select_fusion.1), calls=%async_computation.3 | async-start | bytes 524288 | tf_op jit(solution)/shard_map/all_to_all | solution.py:142
  195.3 20.6 %psum.7 = f32[32,4]{1,0:T(8,128)S(1)} all-reduce(f32[32,4]{1,0:T(8,128)S(1)} %copy-done.31), channel_id=1, replica_groups=mesh['seq'=32,'mp'=8] {'mp'}, use_global_device_ids=true, to_apply=%region_34.35 | all-reduce | flops 128 | bytes 1024 | tf_op jit(solution)/shard_map/psum | solution.py:151
  216.1 2.2 scatter_custom_fusion
  218.3 1.5 scatter_custom_fusion.4
  219.9 2.2 scatter_custom_fusion.1
  222.1 183.0 %reduce-scatter.2.cloned.1.call-done = f32[128,256]{0,1:T(8,128)} async-done(((f32[4096,256]{0,1:T(8,128)}), f32[128,256]{0,1:T(8,128)}) %reduce-scatter.2.cloned.1.call-update) | async-done | bytes 131088 | tf_op jit(solution)/shard_map/reduce_scatter | solution.py:128
  405.1 0.9 convert_element_type.258
  406.2 1.6 scatter_custom_fusion.3
  407.9 1.6 scatter_custom_fusion.2
  (184 shorter events, 19.2 us)
Async XLA Ops:
  7.2 37.2 %copy-start = (bf16[512,1024]{1,0:T(8,128)(2,1)S(1)}, bf16[512,1024]{1,0:T(8,128)(2,1)}, u32[]{:S(2)}) copy-start(bf16[512,1024]{1,0:T(8,128)(2,1)} %param.6) | copy-start | bytes 3145732
  7.2 34.8 %copy-start.1 = (s32[128]{0:T(128)S(1)}, s32[128]{0:T(128)}, u32[]{:S(2)}) copy-start(s32[128]{0:T(128)} %param.11) | copy-start | bytes 1540
  7.2 90.3 %all-gather.2.cloned.1.call-start = ((), (), s32[]{:S(2)}) async-start(), calls=%async_computation.5 | async-start | bytes 2162688 | tf_op jit(solution)/shard_map/all_gather | solution.py:67
  47.1 49.6 %all-to-all-start = ((bf16[32,4,1024]{2,1,0:T(4,128)(2,1)}), bf16[32,4,1024]{2,1,0:T(4,128)(2,1)S(1)}, u32[]{:S(2)}, u32[]{:S(2)}) async-start(bf16[32,4,1024]{2,1,0:T(4,128)(2,1)} %broadcast_select_fusion), calls=%async_computation | async-start | bytes 524288 | tf_op jit(solution)/shard_map/all_to_all | solution.py:49
  97.5 1.9 copy-start.3
  105.9 2.3 copy-start.21
  106.2 3.2 copy-start.5
  106.6 3.8 copy-start.7
  106.9 4.4 %copy-start.9 = (bf16[64,4096]{1,0:T(8,128)(2,1)}, bf16[64,4096]{1,0:T(8,128)(2,1)S(1)}, u32[]{:S(2)}) copy-start(bf16[64,4096]{1,0:T(8,128)(2,1)S(1)} %get-tuple-element.38) | copy-start | bytes 1572868
  107.3 4.9 %copy-start.11 = (bf16[64,4096]{1,0:T(8,128)(2,1)}, bf16[64,4096]{1,0:T(8,128)(2,1)S(1)}, u32[]{:S(2)}) copy-start(bf16[64,4096]{1,0:T(8,128)(2,1)S(1)} %get-tuple-element.36) | copy-start | bytes 1572868
  107.6 5.5 %copy-start.13 = (bf16[64,4096]{1,0:T(8,128)(2,1)}, bf16[64,4096]{1,0:T(8,128)(2,1)S(1)}, u32[]{:S(2)}) copy-start(bf16[64,4096]{1,0:T(8,128)(2,1)S(1)} %get-tuple-element.34) | copy-start | bytes 1572868
  107.9 6.1 %copy-start.15 = (bf16[64,4096]{1,0:T(8,128)(2,1)}, bf16[64,4096]{1,0:T(8,128)(2,1)S(1)}, u32[]{:S(2)}) copy-start(bf16[64,4096]{1,0:T(8,128)(2,1)S(1)} %get-tuple-element.32) | copy-start | bytes 1572868
  108.2 3.1 copy-start.4
  108.2 6.7 %copy-start.17 = (bf16[64,4096]{1,0:T(8,128)(2,1)}, bf16[64,4096]{1,0:T(8,128)(2,1)S(1)}, u32[]{:S(2)}) copy-start(bf16[64,4096]{1,0:T(8,128)(2,1)S(1)} %get-tuple-element.30) | copy-start | bytes 1572868
  115.9 15.1 %copy-start.2 = (f32[512]{0:T(512)S(1)}, f32[512]{0:T(512)}, u32[]{:S(2)}) copy-start(f32[512]{0:T(512)} %param.10) | copy-start | bytes 6148
  121.1 20.7 %all-to-all-start.1 = ((bf16[32,4,1024]{2,1,0:T(4,128)(2,1)}), bf16[32,4,1024]{2,1,0:T(4,128)(2,1)}, u32[]{:S(2)}, u32[]{:S(2)}) async-start(bf16[32,4,1024]{2,1,0:T(4,128)(2,1)} %broadcast_select_fusion.2), calls=%async_computation.1 | async-start | bytes 524288 | tf_op jit(solution)/shard_map/all_to_all | solution.py:141
  132.4 12.3 %copy-start.29 = (f32[32,4]{1,0:T(8,128)}, f32[32,4]{1,0:T(8,128)S(1)}, u32[]{:S(2)}) copy-start(f32[32,4]{1,0:T(8,128)S(1)} %reshape.969) | copy-start | bytes 1540
  144.7 16.3 %all-to-all-start.2 = ((bf16[32,4,1024]{2,1,0:T(4,128)(2,1)}), bf16[32,4,1024]{2,1,0:T(4,128)(2,1)}, u32[]{:S(2)}, u32[]{:S(2)}) async-start(bf16[32,4,1024]{2,1,0:T(4,128)(2,1)} %get-tuple-element.50), calls=%async_computation.2 | async-start | bytes 524288 | tf_op jit(solution)/shard_map/all_to_all | solution.py:50
  150.2 254.9 %reduce-scatter.2.cloned.1.call-start = ((), (), s32[]{:S(2)}) async-start(), calls=%async_computation.6 | async-start | bytes 4325376 | tf_op jit(solution)/shard_map/reduce_scatter | solution.py:128
  162.7 5.0 %copy-start.32 = (bf16[64,128]{1,0:T(8,128)(2,1)S(1)}, bf16[64,128]{1,0:T(8,128)(2,1)}, u32[]{:S(2)}) copy-start(bf16[64,128]{1,0:T(8,128)(2,1)} %get-tuple-element.125) | copy-start | bytes 49156
  162.7 5.0 %copy-start.33 = (bf16[64,128]{1,0:T(8,128)(2,1)S(1)}, bf16[64,128]{1,0:T(8,128)(2,1)}, u32[]{:S(2)}) copy-start(bf16[64,128]{1,0:T(8,128)(2,1)} %get-tuple-element.127) | copy-start | bytes 49156
  162.7 5.0 %copy-start.34 = (bf16[64,128]{1,0:T(8,128)(2,1)S(1)}, bf16[64,128]{1,0:T(8,128)(2,1)}, u32[]{:S(2)}) copy-start(bf16[64,128]{1,0:T(8,128)(2,1)} %get-tuple-element.129) | copy-start | bytes 49156
  162.7 5.0 %copy-start.35 = (bf16[64,128]{1,0:T(8,128)(2,1)S(1)}, bf16[64,128]{1,0:T(8,128)(2,1)}, u32[]{:S(2)}) copy-start(bf16[64,128]{1,0:T(8,128)(2,1)} %get-tuple-element.131) | copy-start | bytes 49156
  162.7 5.0 %copy-start.36 = (bf16[64,128]{1,0:T(8,128)(2,1)S(1)}, bf16[64,128]{1,0:T(8,128)(2,1)}, u32[]{:S(2)}) copy-start(bf16[64,128]{1,0:T(8,128)(2,1)} %get-tuple-element.133) | copy-start | bytes 49156
  162.8 5.0 %copy-start.37 = (bf16[64,128]{1,0:T(8,128)(2,1)S(1)}, bf16[64,128]{1,0:T(8,128)(2,1)}, u32[]{:S(2)}) copy-start(bf16[64,128]{1,0:T(8,128)(2,1)} %get-tuple-element.135) | copy-start | bytes 49156
  162.8 5.0 %copy-start.38 = (bf16[64,128]{1,0:T(8,128)(2,1)S(1)}, bf16[64,128]{1,0:T(8,128)(2,1)}, u32[]{:S(2)}) copy-start(bf16[64,128]{1,0:T(8,128)(2,1)} %get-tuple-element.137) | copy-start | bytes 49156
  162.8 5.0 %copy-start.39 = (bf16[64,128]{1,0:T(8,128)(2,1)S(1)}, bf16[64,128]{1,0:T(8,128)(2,1)}, u32[]{:S(2)}) copy-start(bf16[64,128]{1,0:T(8,128)(2,1)} %get-tuple-element.139) | copy-start | bytes 49156
  162.8 5.2 %copy-start.22 = (bf16[64,4096]{1,0:T(8,128)(2,1)S(1)}, bf16[64,4096]{1,0:T(8,128)(2,1)}, u32[]{:S(2)}) copy-start(bf16[64,4096]{1,0:T(8,128)(2,1)} %copy-done.21) | copy-start | bytes 1572868
  167.7 1.6 copy-start.6
  168.0 2.6 copy-start.8
  169.3 2.6 copy-start.10
  170.6 2.6 copy-start.12
  171.9 2.6 copy-start.14
  173.2 2.6 copy-start.16
  174.5 2.6 copy-start.18
  175.8 2.6 copy-start.20
  183.5 2.9 copy-start.23
  183.5 3.2 copy-start.24
  184.9 2.1 copy-start.25
  186.4 1.0 copy-start.26
  186.7 1.1 copy-start.27
  187.0 1.1 copy-start.28
  188.5 6.8 %copy-start.19 = (bf16[32,4,1024]{2,1,0:T(4,128)(2,1)S(1)}, bf16[32,4,1024]{2,1,0:T(4,128)(2,1)}, u32[]{:S(2)}) copy-start(bf16[32,4,1024]{2,1,0:T(4,128)(2,1)} %get-tuple-element.51) | copy-start | bytes 786436
  188.5 6.9 %copy-start.31 = (f32[32,4]{1,0:T(8,128)S(1)}, f32[32,4]{1,0:T(8,128)}, u32[]{:S(2)}) copy-start(f32[32,4]{1,0:T(8,128)} %get-tuple-element.49) | copy-start | bytes 1540
  188.5 27.5 %copy-start.30 = (f32[32,4]{1,0:T(8,128)S(1)}, f32[32,4]{1,0:T(8,128)}, u32[]{:S(2)}) copy-start(f32[32,4]{1,0:T(8,128)} %copy-done.29) | copy-start | bytes 1540
  190.4 29.4 %all-to-all-start.3 = ((bf16[32,4,1024]{2,1,0:T(4,128)(2,1)}), bf16[32,4,1024]{2,1,0:T(4,128)(2,1)S(1)}, u32[]{:S(2)}, u32[]{:S(2)}) async-start(bf16[32,4,1024]{2,1,0:T(4,128)(2,1)} %broadcast_select_fusion.1), calls=%async_computation.3 | async-start | bytes 524288 | tf_op jit(solution)/shard_map/all_to_all | solution.py:142
Sparse Core Ops, SparseCore 0:
  13.8 81.9 all-gather.1
  183.6 221.4 reduce-scatter.1
where the time goes:
time: 418 us; the launch traced here: 416 us
  waiting for transfers between devices  197 us (47%)
  other arithmetic  62.7 us (15%)
  blocking collectives  44.4 us (11%)
  local copies, waits for them, and re-layouts  36.6 us (9%)
  matrix products  36.3 us (9%)
  starting transfers between devices  24.2 us (6%)
  between operations  14.9 us (4%)
    reduce_scatter x1, waiting for transfers between devices, shards(): lax.psum_scatter(jnp.concatenate([key_part.reshape(lax.axis_size('seq') *...  183 us
    select_n x1, other arithmetic, shards(): jnp.where(key_slot < counts[key_source], offsets[key_source] + key_slot,...  31.4 us
    unnamed x1, blocking collectives  23.8 us
    psum x1, blocking collectives, shards(): feature_sum = lax.psum(partial_sums, 'mp')  20.6 us
    dot_general x8, matrix products, shards(): lax.dot_general(grad_head, value_head, contract, preferred_element_type=j...  10.3 us
    all_to_all x1, starting transfers between devices, shards(): lax.all_to_all(slots_back(attended_all), 'seq', split_axis=0, concat_axis...  9.92 us
    all_to_all x1, waiting for transfers between devices, shards(): lax.all_to_all(grad_send, 'seq', split_axis=0, concat_axis=0, tiled=True)  9.83 us
  transfers between devices with their start and end apart: 6, of which 3 were waited for; matrix products, arithmetic and copies ran while one was open for 18% of the time, Pallas kernels for 0%

commit v1 on v0

--- a/solution.py
+++ b/solution.py
@@ -148,7 +148,7 @@
     mixed = place_rows((router[:, :, None] * out_float).astype(jnp.bfloat16), positions, tok_rows)
     query_grad = place_rows(dquery_back, positions, tok_rows)
     partial_sums = jnp.sum(cot_rows.astype(jnp.float32) * out_float, axis=2)
-    feature_sum = lax.psum(partial_sums, "mp")
+    feature_sum = jax.lax.all_gather(partial_sums, "mp").sum(axis=0)
     router_terms = (router * (1.0 - router) * feature_sum).reshape(-1)
     router_grad = (
         jnp.zeros((tok_rows,), jnp.float32).at[positions.reshape(-1)].set(router_terms, mode="drop")

time: 418 us -> 436 us (1.043)
  waiting for transfers between devices: 197 us -> 219 us
  blocking collectives: 44.4 us -> 35.8 us
    psum x1 -> x0, blocking collectives: 20.6 us -> none  [shards(): feature_sum = lax.psum(partial_sums, 'mp')]
    all_gather x0 -> x1, blocking collectives: none -> 12 us  [shards(): feature_sum = jax.lax.all_gather(partial_sums, 'mp').sum(axis=0)]
    reduce_scatter x1, waiting for transfers between devices: 183 us -> 194 us  [shards(): lax.psum_scatter(jnp.concatenate([key_part.reshape(lax.axis_size('seq') *...]
    all_to_all x1, waiting for transfers between devices: 0.01 us -> 8.85 us  [shards(): lax.all_to_all(slots_back(dquery_all), 'seq', split_axis=0, concat_axis=0...]
  transfers between devices with their start and end apart: 6 -> 6, of which waited for: 3 -> 4; matrix products, arithmetic and copies ran while one was open for 18% -> 18% of each run, Pallas kernels for 0% -> 0%
where the time goes in v1:
time: 436 us; the launch traced here: 435 us
  waiting for transfers between devices  219 us (50%)
  other arithmetic  64.4 us (15%)
  local copies, waits for them, and re-layouts  39.6 us (9%)
  matrix products  36.3 us (8%)
  blocking collectives  35.8 us (8%)
  starting transfers between devices  24.3 us (6%)
  between operations  14.9 us (3%)
    reduce_scatter x1, waiting for transfers between devices, shards(): lax.psum_scatter(jnp.concatenate([key_part.reshape(lax.axis_size('seq') *...  194 us
    select_n x1, other arithmetic, shards(): jnp.where(key_slot < counts[key_source], offsets[key_source] + key_slot,...  31.2 us
    unnamed x1, blocking collectives  23.8 us
    all_gather x1, blocking collectives, shards(): feature_sum = jax.lax.all_gather(partial_sums, 'mp').sum(axis=0)  12 us
    all_to_all x1, waiting for transfers between devices, shards(): lax.all_to_all(grad_send, 'seq', split_axis=0, concat_axis=0, tiled=True)  11.7 us
    dot_general x8, matrix products, shards(): lax.dot_general(grad_head, value_head, contract, preferred_element_type=j...  10.3 us
    all_to_all x1, starting transfers between devices, shards(): lax.all_to_all(slots_back(attended_all), 'seq', split_axis=0, concat_axis...  9.77 us
    all_to_all x1, waiting for transfers between devices, shards(): lax.all_to_all(slots_back(dquery_all), 'seq', split_axis=0, concat_axis=0...  8.85 us
  transfers between devices with their start and end apart: 6, of which 4 were waited for; matrix products, arithmetic and copies ran while one was open for 18% of the time, Pallas kernels for 0%

profile of v1, /device:TPU:4, one launch (start us, length us, event | category | flops | bytes accessed | tf_op | source)
XLA Modules:
  0.0 434.7 jit_solution(6151515626174869011)
XLA Ops:
  7.2 1.9 compare_select_fusion.32
  9.8 1.6 gather_fusion.5
  11.3 1.6 gather_fusion.6
  13.7 1.3 dynamic-slice
  15.0 1.4 dynamic-update-slice
  16.4 23.8 %all-reduce = s32[32]{0:T(128)S(1)} all-reduce(s32[32]{0:T(128)S(1)} %dynamic-update-slice), channel_id=1, replica_groups=mesh['seq'=32,'mp'=8] {'seq'}, use_global_device_ids=true, to_apply=%add | all-reduce | flops 32 | bytes 256
  41.9 1.2 gather_fusion
  44.3 0.9 gather_fusion.2
  45.4 1.3 broadcast_select_fusion.3
  46.8 0.9 broadcast_select_fusion
  47.7 3.9 all-to-all-start
  55.2 4.3 compare_select_fusion.21
  59.5 4.3 compare_select_fusion.20
  66.4 31.2 %fusion.70 = s32[4096]{0:T(1024)S(1)} fusion(pred[4096]{0:T(1024)(128)(4,1)S(1)} %compare_reduce_fusion, pred[4096]{0:T(1024)(128)(4,1)S(1)} %compare_reduce_fusion.1, pred[4096]{0:T(1024)(128)(4,1)S(1)} %compare_reduce_fusion.2, pred[4096]{0:T(1024)(128)(4,1)S(1)} %compare_reduce_fusion.3, pred[4096]{0:T(1024)(128)(4,1)S(1)} %compare_reduce_fusion.4, ...), kind=kLoop, calls=%fused_computation.237 | loop fusion | flops 241664 | bytes 151752 | tf_op jit(solution)/shard_map/jit(_where)/select_n | solution.py:71
  98.4 1.9 convolution_multiply_fusion.1
  103.2 1.3 fusion.41
  104.5 1.9 fusion.49
  109.1 1.2 constant_dynamic-update-slice_fusion.7
  110.3 0.9 constant_dynamic-update-slice_fusion.6
  111.2 0.9 constant_dynamic-update-slice_fusion.5
  112.1 0.9 constant_dynamic-update-slice_fusion.4
  113.0 0.9 constant_dynamic-update-slice_fusion.3
  113.9 0.9 constant_dynamic-update-slice_fusion.2
  114.9 0.9 constant_dynamic-update-slice_fusion.1
  115.8 0.9 constant_dynamic-update-slice_fusion
  116.7 1.6 gather_fusion.7
  118.3 1.1 reshape.809
  119.4 0.9 broadcast_select_fusion.2
  120.3 9.8 %all-to-all-start.1 = ((bf16[32,4,1024]{2,1,0:T(4,128)(2,1)}), bf16[32,4,1024]{2,1,0:T(4,128)(2,1)S(1)}, u32[]{:S(2)}, u32[]{:S(2)}) async-start(bf16[32,4,1024]{2,1,0:T(4,128)(2,1)} %broadcast_select_fusion.2), calls=%async_computation.1 | async-start | bytes 524288 | tf_op jit(solution)/shard_map/all_to_all | solution.py:141
  130.0 3.1 gather_fusion.8
  133.2 1.9 reshape.893
  135.1 1.3 gather_fusion.1
  136.3 4.5 %all-to-all-done.1 = bf16[32,4,1024]{2,1,0:T(4,128)(2,1)S(1)} async-done(((bf16[32,4,1024]{2,1,0:T(4,128)(2,1)}), bf16[32,4,1024]{2,1,0:T(4,128)(2,1)S(1)}, u32[]{:S(2)}, u32[]{:S(2)}) %all-to-all-start.1) | async-done | bytes 262176 | tf_op jit(solution)/shard_map/all_to_all | solution.py:141
  140.8 1.9 fusion.51
  143.5 12.0 %all-gather.1 = f32[8,32,4]{1,2,0:T(4,128)} all-gather(f32[1,32,4]{1,2,0:T(4,128)S(1)} %bitcast.171), channel_id=2, replica_groups=mesh['seq'=32,'mp'=8] {'mp'}, dimensions={0}, use_global_device_ids=true | all-gather | bytes 4608 | tf_op jit(solution)/shard_map/all_gather | solution.py:151
  159.1 2.1 select_convert_fusion
  161.2 5.4 %all-to-all-start.2 = ((bf16[32,4,1024]{2,1,0:T(4,128)(2,1)}), bf16[32,4,1024]{2,1,0:T(4,128)(2,1)}, u32[]{:S(2)}, u32[]{:S(2)}) async-start(bf16[32,4,1024]{2,1,0:T(4,128)(2,1)} %get-tuple-element.53), calls=%async_computation.2 | async-start | bytes 524288 | tf_op jit(solution)/shard_map/all_to_all | solution.py:50
  167.6 11.7 %all-to-all-done.2 = bf16[32,4,1024]{2,1,0:T(4,128)(2,1)} async-done(((bf16[32,4,1024]{2,1,0:T(4,128)(2,1)}), bf16[32,4,1024]{2,1,0:T(4,128)(2,1)}, u32[]{:S(2)}, u32[]{:S(2)}) %all-to-all-start.2) | async-done | bytes 262176 | tf_op jit(solution)/shard_map/all_to_all | solution.py:50
  179.3 1.0 reshape.668
  180.3 0.8 gather_fusion.9
  181.3 4.9 %convolution_bitcast_fusion = f32[4096,128]{0,1:T(8,128)S(1)} fusion(bf16[64,8,128]{2,1,0:T(8,128)(2,1)S(1)} %bitcast.168, bf16[8,64,4096]{2,1,0:T(8,128)(2,1)} %copy-done.4), kind=kOutput, calls=%fused_computation.32 | convolution fusion | flops 536870912 | bytes 6422528 | tf_op jit(solution)/shard_map/hgbk,bhgd->khd/dot_general | solution.py:125
  186.5 1.3 bitcast_dynamic-update-slice_fusion.15
  187.8 1.3 bitcast_dynamic-update-slice_fusion.14
  189.1 1.3 bitcast_dynamic-update-slice_fusion.13
  190.4 1.3 bitcast_dynamic-update-slice_fusion.12
  191.7 1.3 bitcast_dynamic-update-slice_fusion.11
  193.0 1.3 bitcast_dynamic-update-slice_fusion.10
  194.3 1.3 bitcast_dynamic-update-slice_fusion.9
  195.6 1.3 bitcast_dynamic-update-slice_fusion.8
  196.9 2.6 convolution_bitcast_fusion.1
  199.6 2.4 pad_maximum_fusion
  202.0 1.4 fusion.33
  203.4 1.4 fusion.32
  207.0 0.9 gather_fusion.10
  208.0 0.9 broadcast_select_fusion.1
  208.9 4.9 %all-to-all-start.3 = ((bf16[32,4,1024]{2,1,0:T(4,128)(2,1)}), bf16[32,4,1024]{2,1,0:T(4,128)(2,1)S(1)}, u32[]{:S(2)}, u32[]{:S(2)}) async-start(bf16[32,4,1024]{2,1,0:T(4,128)(2,1)} %broadcast_select_fusion.1), calls=%async_computation.3 | async-start | bytes 524288 | tf_op jit(solution)/shard_map/all_to_all | solution.py:142
  214.1 1.7 scatter_custom_fusion.4
  215.8 2.2 scatter_custom_fusion
  218.0 8.8 %all-to-all-done.3 = bf16[32,4,1024]{2,1,0:T(4,128)(2,1)S(1)} async-done(((bf16[32,4,1024]{2,1,0:T(4,128)(2,1)}), bf16[32,4,1024]{2,1,0:T(4,128)(2,1)S(1)}, u32[]{:S(2)}, u32[]{:S(2)}) %all-to-all-start.3) | async-done | bytes 262176 | tf_op jit(solution)/shard_map/all_to_all | solution.py:142
  226.9 2.2 scatter_custom_fusion.1
  229.1 194.3 %reduce-scatter.2.cloned.1.call-done = f32[128,256]{0,1:T(8,128)} async-done(((f32[4096,256]{0,1:T(8,128)}), f32[128,256]{0,1:T(8,128)}) %reduce-scatter.2.cloned.1.call-update) | async-done | bytes 131088 | tf_op jit(solution)/shard_map/reduce_scatter | solution.py:128
  423.4 0.9 convert_element_type.258
  424.6 1.6 scatter_custom_fusion.3
  426.2 1.6 scatter_custom_fusion.2
  (191 shorter events, 25.4 us)
Async XLA Ops:
  7.2 37.2 %copy-start = (bf16[512,1024]{1,0:T(8,128)(2,1)S(1)}, bf16[512,1024]{1,0:T(8,128)(2,1)}, u32[]{:S(2)}) copy-start(bf16[512,1024]{1,0:T(8,128)(2,1)} %param.6) | copy-start | bytes 3145732
  7.2 34.8 %copy-start.1 = (s32[128]{0:T(128)S(1)}, s32[128]{0:T(128)}, u32[]{:S(2)}) copy-start(s32[128]{0:T(128)} %param.11) | copy-start | bytes 1540
  7.2 91.2 %all-gather.4.cloned.1.call-start = ((), (), s32[]{:S(2)}) async-start(), calls=%async_computation.5 | async-start | bytes 2162688 | tf_op jit(solution)/shard_map/all_gather | solution.py:67
  46.8 8.4 %copy-start.31 = (pred[32,4]{1,0:T(8,128)(4,1)}, pred[32,4]{1,0:T(8,128)(4,1)S(1)}, u32[]{:S(2)}) copy-start(pred[32,4]{1,0:T(8,128)(4,1)S(1)} %copy.37) | copy-start | bytes 388
  47.7 49.9 %all-to-all-start = ((bf16[32,4,1024]{2,1,0:T(4,128)(2,1)}), bf16[32,4,1024]{2,1,0:T(4,128)(2,1)S(1)}, u32[]{:S(2)}, u32[]{:S(2)}) async-start(bf16[32,4,1024]{2,1,0:T(4,128)(2,1)} %broadcast_select_fusion), calls=%async_computation | async-start | bytes 524288 | tf_op jit(solution)/shard_map/all_to_all | solution.py:49
  53.7 46.6 %copy-start.41 = (s32[1024]{0:T(1024)}, s32[1024]{0:T(1024)S(1)}, u32[]{:S(2)}) copy-start(s32[1024]{0:T(1024)S(1)} %pad_clamp_fusion.2) | copy-start | bytes 12292
  98.4 1.9 copy-start.3
  106.7 2.3 copy-start.21
  107.1 3.2 copy-start.5
  107.4 3.8 copy-start.7
  107.7 4.4 %copy-start.9 = (bf16[64,4096]{1,0:T(8,128)(2,1)}, bf16[64,4096]{1,0:T(8,128)(2,1)S(1)}, u32[]{:S(2)}) copy-start(bf16[64,4096]{1,0:T(8,128)(2,1)S(1)} %get-tuple-element.40) | copy-start | bytes 1572868
  108.1 5.0 %copy-start.11 = (bf16[64,4096]{1,0:T(8,128)(2,1)}, bf16[64,4096]{1,0:T(8,128)(2,1)S(1)}, u32[]{:S(2)}) copy-start(bf16[64,4096]{1,0:T(8,128)(2,1)S(1)} %get-tuple-element.38) | copy-start | bytes 1572868
  108.4 5.5 %copy-start.13 = (bf16[64,4096]{1,0:T(8,128)(2,1)}, bf16[64,4096]{1,0:T(8,128)(2,1)S(1)}, u32[]{:S(2)}) copy-start(bf16[64,4096]{1,0:T(8,128)(2,1)S(1)} %get-tuple-element.36) | copy-start | bytes 1572868
  108.7 6.1 %copy-start.15 = (bf16[64,4096]{1,0:T(8,128)(2,1)}, bf16[64,4096]{1,0:T(8,128)(2,1)S(1)}, u32[]{:S(2)}) copy-start(bf16[64,4096]{1,0:T(8,128)(2,1)S(1)} %get-tuple-element.34) | copy-start | bytes 1572868
  109.1 3.1 copy-start.4
  109.1 6.7 %copy-start.17 = (bf16[64,4096]{1,0:T(8,128)(2,1)}, bf16[64,4096]{1,0:T(8,128)(2,1)S(1)}, u32[]{:S(2)}) copy-start(bf16[64,4096]{1,0:T(8,128)(2,1)S(1)} %get-tuple-element.32) | copy-start | bytes 1572868
  115.8 3.6 copy-start.29
  119.3 15.7 %copy-start.2 = (f32[512]{0:T(512)S(1)}, f32[512]{0:T(512)}, u32[]{:S(2)}) copy-start(f32[512]{0:T(512)} %param.10) | copy-start | bytes 6148
  120.3 20.6 %all-to-all-start.1 = ((bf16[32,4,1024]{2,1,0:T(4,128)(2,1)}), bf16[32,4,1024]{2,1,0:T(4,128)(2,1)S(1)}, u32[]{:S(2)}, u32[]{:S(2)}) async-start(bf16[32,4,1024]{2,1,0:T(4,128)(2,1)} %broadcast_select_fusion.2), calls=%async_computation.1 | async-start | bytes 524288 | tf_op jit(solution)/shard_map/all_to_all | solution.py:141
  161.2 18.1 %all-to-all-start.2 = ((bf16[32,4,1024]{2,1,0:T(4,128)(2,1)}), bf16[32,4,1024]{2,1,0:T(4,128)(2,1)}, u32[]{:S(2)}, u32[]{:S(2)}) async-start(bf16[32,4,1024]{2,1,0:T(4,128)(2,1)} %get-tuple-element.53), calls=%async_computation.2 | async-start | bytes 524288 | tf_op jit(solution)/shard_map/all_to_all | solution.py:50
  166.6 256.8 %reduce-scatter.2.cloned.1.call-start = ((), (), s32[]{:S(2)}) async-start(), calls=%async_computation.6 | async-start | bytes 4325376 | tf_op jit(solution)/shard_map/reduce_scatter | solution.py:128
  181.2 5.0 %copy-start.32 = (bf16[64,128]{1,0:T(8,128)(2,1)S(1)}, bf16[64,128]{1,0:T(8,128)(2,1)}, u32[]{:S(2)}) copy-start(bf16[64,128]{1,0:T(8,128)(2,1)} %get-tuple-element.126) | copy-start | bytes 49156
  181.2 5.0 %copy-start.33 = (bf16[64,128]{1,0:T(8,128)(2,1)S(1)}, bf16[64,128]{1,0:T(8,128)(2,1)}, u32[]{:S(2)}) copy-start(bf16[64,128]{1,0:T(8,128)(2,1)} %get-tuple-element.128) | copy-start | bytes 49156
  181.2 5.0 %copy-start.34 = (bf16[64,128]{1,0:T(8,128)(2,1)S(1)}, bf16[64,128]{1,0:T(8,128)(2,1)}, u32[]{:S(2)}) copy-start(bf16[64,128]{1,0:T(8,128)(2,1)} %get-tuple-element.130) | copy-start | bytes 49156
  181.2 5.0 %copy-start.35 = (bf16[64,128]{1,0:T(8,128)(2,1)S(1)}, bf16[64,128]{1,0:T(8,128)(2,1)}, u32[]{:S(2)}) copy-start(bf16[64,128]{1,0:T(8,128)(2,1)} %get-tuple-element.132) | copy-start | bytes 49156
  181.2 5.0 %copy-start.36 = (bf16[64,128]{1,0:T(8,128)(2,1)S(1)}, bf16[64,128]{1,0:T(8,128)(2,1)}, u32[]{:S(2)}) copy-start(bf16[64,128]{1,0:T(8,128)(2,1)} %get-tuple-element.134) | copy-start | bytes 49156
  181.2 5.0 %copy-start.37 = (bf16[64,128]{1,0:T(8,128)(2,1)S(1)}, bf16[64,128]{1,0:T(8,128)(2,1)}, u32[]{:S(2)}) copy-start(bf16[64,128]{1,0:T(8,128)(2,1)} %get-tuple-element.136) | copy-start | bytes 49156
  181.2 5.0 %copy-start.38 = (bf16[64,128]{1,0:T(8,128)(2,1)S(1)}, bf16[64,128]{1,0:T(8,128)(2,1)}, u32[]{:S(2)}) copy-start(bf16[64,128]{1,0:T(8,128)(2,1)} %get-tuple-element.138) | copy-start | bytes 49156
  181.2 5.0 %copy-start.39 = (bf16[64,128]{1,0:T(8,128)(2,1)S(1)}, bf16[64,128]{1,0:T(8,128)(2,1)}, u32[]{:S(2)}) copy-start(bf16[64,128]{1,0:T(8,128)(2,1)} %get-tuple-element.140) | copy-start | bytes 49156
  181.3 5.2 %copy-start.22 = (bf16[64,4096]{1,0:T(8,128)(2,1)S(1)}, bf16[64,4096]{1,0:T(8,128)(2,1)}, u32[]{:S(2)}) copy-start(bf16[64,4096]{1,0:T(8,128)(2,1)} %copy-done.21) | copy-start | bytes 1572868
  186.2 1.6 copy-start.6
  186.5 2.6 copy-start.8
  187.8 2.6 copy-start.10
  189.1 2.6 copy-start.12
  190.4 2.6 copy-start.14
  191.7 2.6 copy-start.16
  193.0 2.6 copy-start.18
  194.3 2.6 copy-start.20
  202.0 2.9 copy-start.23
  202.0 3.2 copy-start.24
  203.4 2.1 copy-start.25
  204.9 1.0 copy-start.26
  205.2 1.1 copy-start.27
  205.5 1.1 copy-start.28
  206.7 1.3 copy-start.30
  207.0 6.8 %copy-start.40 = (s32[32,4]{0,1:T(4,128)S(1)}, s32[32,4]{0,1:T(4,128)}, u32[]{:S(2)}) copy-start(s32[32,4]{0,1:T(4,128)} %get-tuple-element.49) | copy-start | bytes 1540
  207.0 7.0 %copy-start.19 = (bf16[32,4,1024]{2,1,0:T(4,128)(2,1)S(1)}, bf16[32,4,1024]{2,1,0:T(4,128)(2,1)}, u32[]{:S(2)}) copy-start(bf16[32,4,1024]{2,1,0:T(4,128)(2,1)} %get-tuple-element.54) | copy-start | bytes 786436
  208.9 17.9 %all-to-all-start.3 = ((bf16[32,4,1024]{2,1,0:T(4,128)(2,1)}), bf16[32,4,1024]{2,1,0:T(4,128)(2,1)S(1)}, u32[]{:S(2)}, u32[]{:S(2)}) async-start(bf16[32,4,1024]{2,1,0:T(4,128)(2,1)} %broadcast_select_fusion.1), calls=%async_computation.3 | async-start | bytes 524288 | tf_op jit(solution)/shard_map/all_to_all | solution.py:142
Sparse Core Ops, SparseCore 0:
  13.8 81.0 all-gather.3
  202.1 221.2 reduce-scatter.1
